TPU v7x, 32 devices: a whole 2x2x4 slice. The times are simulated.
32 devices in a mesh: groups: 2 (over x), ctx: 16 (over z, y, core).
Axes of the slice: x: 2, y: 2, z: 4, core: 2. Of those that a mesh axis runs over, the one named last changes fastest.
Arguments:
- queries: bfloat16 [4096, 1024], P(('groups', 'ctx')), parts along dimension 0, may hold values from -27 to 27
- keys: bfloat16 [4096, 1024], P(('groups', 'ctx')), parts along dimension 0, may hold values from -6 to 6
- values: bfloat16 [4096, 1024], P(('groups', 'ctx')), parts along dimension 0, may hold values from -6 to 6
- resid: bfloat16 [4096, 2048], P(('groups', 'ctx')), parts along dimension 0, may hold values from -6 to 6
- out_proj: bfloat16 [1024, 2048], replicated, may hold values from -0.1875 to 0.1875
- norm_gain: float32 [2048], replicated, may hold values from 0.25 to 1.75
- up_proj: bfloat16 [2048, 4096], P(None, 'ctx'), may hold values from -0.125 to 0.125
- down_proj: bfloat16 [2048, 4096], P(None, 'ctx'), may hold values from -0.09375 to 0.09375
- router: bfloat16 [2048, 2], replicated, may hold values from -0.125 to 0.125
- expert_ids: int32 [4096, 1], P(('groups', 'ctx')), parts along dimension 0, may hold values from 0 to 1; in each aligned block of 128 rows (0 to 127, 128 to 255, ...) at most 80 rows name the same one
- expert_in: bfloat16 [16, 2048, 512], P('ctx'), may hold values from -0.125 to 0.125
- expert_out: bfloat16 [16, 512, 2048], P('ctx'), may hold values from -0.09375 to 0.09375
Outputs:
- layer_out: bfloat16 [4096, 2048], P(('groups', 'ctx')), parts along dimension 0
There are 2 independent parts, one for each index of `groups`. A program takes and returns all parts, laid end to end along the dimension named above; an argument that names none is the same for every part. Nothing has to cross between parts.
Inputs may be any that keep to these rules, and one draw needn't show every extreme that they name: `expert_ids`: among the 128 tokens of one index of ctx, at most 80 name the same expert; in every draw some index of ctx has 80 tokens naming one expert.
All inputs are finite; a program needn't handle non-finite values.
Results may differ from a plain program's by a relative error of at most 0.0075.
Values may be sent and summed in bfloat16 or wider, within the bound.
No kernel may reach another device: no remote copies, remote signals or barrier semaphores. Data moves between devices by JAX's collectives and lax.ppermute only.
A program may use at most 192 MiB of HBM per device.

v0:
```python
import jax
import jax.numpy as jnp
from jax import lax
from jax.sharding import PartitionSpec as P

DH = 128
SPLIT = 8
NEG_FILL = -1e30
EPSILON = 1e-06


def from_partner(array, axis, apart):
    return lax.ppermute(array, axis, [(i, i ^ 1 << apart) for i in range(lax.axis_size(axis))])


def update_state(state, query_rows, query_offset, key_block, value_block, key_offset):
    maxima, totals, numer = state
    count_query = query_rows.shape[0]
    count_keys = key_block.shape[0]
    head_count = query_rows.shape[1] // DH
    query_heads = query_rows.reshape(count_query, head_count, DH)
    key_heads = key_block.reshape(count_keys, head_count, DH)
    value_heads = value_block.reshape(count_keys, head_count, DH)
    scores = jnp.einsum(
        "qhd,khd->hqk", query_heads, key_heads, preferred_element_type=jnp.float32
    ) * DH ** (-0.5)
    query_positions = query_offset + jnp.arange(count_query, dtype=jnp.int32)
    key_positions = key_offset + jnp.arange(count_keys, dtype=jnp.int32)
    visible = (key_positions[None, :] <= query_positions[:, None])[None]
    masked = jnp.where(visible, scores, NEG_FILL)
    new_max = jnp.maximum(maxima, jnp.max(masked, axis=2))
    weights = jnp.where(visible, jnp.exp(masked - new_max[..., None]), 0.0)
    factor = jnp.exp(maxima - new_max)
    totals = totals * factor + jnp.sum(weights, axis=2)
    numer = numer * factor[..., None] + jnp.einsum(
        "hqk,khd->hqd",
        weights.astype(jnp.bfloat16),
        value_heads,
        preferred_element_type=jnp.float32,
    )
    return (new_max, totals, numer)


def attend(query_sets, keys, values):
    head_count = keys.shape[1] // DH
    initial = []
    for query_rows, query_offset in query_sets:
        count_query = query_rows.shape[0]
        initial.append(
            (
                jnp.full((head_count, count_query), NEG_FILL, jnp.float32),
                jnp.zeros((head_count, count_query), jnp.float32),
                jnp.zeros((head_count, count_query, DH), jnp.float32),
            )
        )
    states = tuple(initial)
    key_offset = jnp.int32(0)
    key_whole = lax.all_gather(keys, "ctx", axis=0, tiled=True)
    value_whole = lax.all_gather(values, "ctx", axis=0, tiled=True)
    total_keys = key_whole.shape[0]
    step_rows = min(total_keys, 1024)
    for begin in range(0, total_keys, step_rows):
        key_block = key_whole[begin : begin + step_rows]
        value_block = value_whole[begin : begin + step_rows]
        block_offset = key_offset + begin
        query_rows, query_offset = query_sets[0]
        needed = block_offset <= query_offset + query_rows.shape[0] - 1
        updated = [
            lax.cond(
                needed,
                lambda carried, rows_now=query_rows, offset_now=query_offset, keys_now=key_block, values_now=value_block, start_now=block_offset: update_state(
                    carried, rows_now, offset_now, keys_now, values_now, start_now
                ),
                lambda carried: carried,
                states[0],
            )
        ]
        states = tuple(updated)
    results = []
    for maxima, totals, numer in states:
        result = (numer / totals[..., None]).astype(jnp.bfloat16)
        results.append(
            jnp.transpose(result, (1, 0, 2)).reshape(result.shape[1], result.shape[0] * DH)
        )
    return results


def body(
    queries,
    keys,
    values,
    resid,
    out_proj,
    norm_gain,
    up_proj,
    down_proj,
    router,
    expert_ids,
    expert_in,
    expert_out,
):
    tok_rows = queries.shape[0]
    width = resid.shape[1]
    live_count = router.shape[1]
    ctx_count = lax.axis_size("ctx")
    device_index = lax.axis_index("ctx")
    base_offset = device_index * tok_rows
    attn = attend([(queries, base_offset)], keys, values)[0]
    mixed = resid.astype(jnp.float32) + jnp.dot(attn, out_proj, preferred_element_type=jnp.float32)
    normed = (
        mixed * lax.rsqrt(jnp.mean(mixed * mixed, axis=1, keepdims=True) + EPSILON) * norm_gain
    ).astype(jnp.bfloat16)
    mlp_blocks = jnp.stack([up_proj, down_proj], 0)
    for level in range(live_count.bit_length() - 1):
        other_block = from_partner(mlp_blocks, "ctx", level)
        mlp_blocks = jnp.concatenate([mlp_blocks, other_block], axis=2)
    slots_per = max(2, 5 * tok_rows // (4 * live_count))
    chosen = expert_ids[:, 0]
    onehot = (chosen[:, None] == jnp.arange(live_count, dtype=jnp.int32)[None, :]).astype(
        jnp.bfloat16
    )
    row_iota = jnp.arange(tok_rows, dtype=jnp.int32)
    strictly_lower = (row_iota[None, :] < row_iota[:, None]).astype(jnp.bfloat16)
    counts_before = jnp.dot(strictly_lower, onehot, preferred_element_type=jnp.float32)
    slot_index = jnp.sum(onehot.astype(jnp.float32) * counts_before, axis=1).astype(jnp.int32)
    target_slot = chosen * slots_per + slot_index
    dispatch_matrix = (
        jnp.arange(live_count * slots_per, dtype=jnp.int32)[:, None] == target_slot[None, :]
    ).astype(jnp.bfloat16)
    packed = jnp.dot(dispatch_matrix, normed, preferred_element_type=jnp.float32).astype(
        jnp.bfloat16
    )
    sending = jnp.broadcast_to(
        packed.reshape(1, live_count, slots_per, width), (SPLIT, live_count, slots_per, width)
    )
    sending = sending.reshape(ctx_count, 1, slots_per, width)
    own_expert = device_index % live_count
    router_column = lax.dynamic_slice_in_dim(router, own_expert, 1, 1)
    weight_in = expert_in[0]
    weight_out = expert_out[0]
    received = lax.all_to_all(sending, "ctx", split_axis=0, concat_axis=1, tiled=True)
    rows = received.reshape(-1, width)
    expert_hidden = jax.nn.gelu(
        jnp.dot(rows, weight_in, preferred_element_type=jnp.float32)
    ).astype(jnp.bfloat16)
    mlp_hidden = jax.nn.gelu(
        jnp.dot(rows, mlp_blocks[0], preferred_element_type=jnp.float32)
    ).astype(jnp.bfloat16)
    gate = jax.nn.sigmoid(jnp.dot(rows, router_column, preferred_element_type=jnp.float32))
    produced = gate * jnp.dot(expert_hidden, weight_out, preferred_element_type=jnp.float32)
    produced = produced + lax.dot_general(
        mlp_hidden, mlp_blocks[1], (((1,), (1,)), ((), ())), preferred_element_type=jnp.float32
    )
    came_back = lax.all_to_all(
        produced.astype(jnp.bfloat16).reshape(received.shape),
        "ctx",
        split_axis=1,
        concat_axis=0,
        tiled=True,
    )
    summed = jnp.sum(
        came_back.astype(jnp.float32).reshape(SPLIT, live_count * slots_per, width), axis=0
    )
    mixture_part = lax.dot_general(
        dispatch_matrix.astype(jnp.float32),
        summed,
        (((0,), (0,)), ((), ())),
        precision=lax.Precision.HIGHEST,
        preferred_element_type=jnp.float32,
    )
    return (mixed + mixture_part).astype(jnp.bfloat16)


def solution(mesh):
    placed = (
        P(("groups", "ctx"), None),
        P(("groups", "ctx"), None),
        P(("groups", "ctx"), None),
        P(("groups", "ctx"), None),
        P(),
        P(),
        P(None, "ctx"),
        P(None, "ctx"),
        P(),
        P(("groups", "ctx"), None),
        P("ctx", None, None),
        P("ctx", None, None),
    )
    return jax.shard_map(
        body, mesh=mesh, in_specs=placed, out_specs=P(("groups", "ctx"), None), check_vma=False
    )
```

profile of v0, /device:TPU:1, one launch (start us, length us, event | category | flops | bytes accessed | tf_op | source)
XLA Modules:
  0.0 418.6 jit_solution(9774764442608556047)
XLA Ops:
  6.5 0.0 copy-start
  6.5 0.0 all-gather.3.cloned.1.call-start
  6.5 1.9 copy.30
  8.5 0.0 all-gather.3.cloned.1.call-update
  8.5 0.0 all-gather.5.cloned.1.call-start
  8.6 1.8 copy.31
  10.4 0.0 all-gather.5.cloned.1.call-update
  10.4 0.9 fusion.63
  11.3 0.7 convert_add_fusion
  12.0 52.5 %all-gather.3.cloned.1.call-done = bf16[2048,1024]{0,1:T(8,128)(2,1)} async-done(((bf16[128,1024]{0,1:T(8,128)(2,1)}), bf16[2048,1024]{0,1:T(8,128)(2,1)}) %all-gather.3.cloned.1.call-update) | async-done | bytes 4194320 | tf_op jit(solution)/shard_map/all_gather | solution.py:58
  64.5 52.8 %all-gather.5.cloned.1.call-done = bf16[2048,1024]{0,1:T(8,128)(2,1)} async-done(((bf16[128,1024]{0,1:T(8,128)(2,1)}), bf16[2048,1024]{0,1:T(8,128)(2,1)}) %all-gather.5.cloned.1.call-update) | async-done | bytes 4194320 | tf_op jit(solution)/shard_map/all_gather | solution.py:59
  117.3 9.7 %conditional.2 = (f32[8,128]{1,0:T(8,128)}, f32[8,128]{1,0:T(8,128)S(1)}, f32[8,128,128]{2,1,0:T(8,128)S(1)}) conditional(s32[]{:T(128)} %convert_element_type.67, () %tuple.20, (s32[]{:T(128)}, bf16[128,1024]{1,0:T(8,128)(2,1)}, bf16[2048,1024]{0,1:T(8,128)(2,1)}, bf16[2048,1024]{0,1:T(8,128)(2,1)}) %tuple.21), branch_computations={%region_0.0_spmd, %region_1.4_spmd} | conditional | flops 550768768 | bytes 44348500 | solution.py:69
  117.3 0.0 copy-start.2
  117.3 0.1 iota_compare_fusion
  117.5 0.0 copy-start.4
  117.5 1.9 slice.24
  119.4 0.7 copy-done.2
  120.1 0.2 slice.25
  120.4 0.0 copy-done.4
  120.4 1.1 fusion
  121.5 0.6 exponential_multiply_fusion
  122.1 2.2 fusion.10
  124.4 2.0 fusion.2
  126.3 0.7 fusion.19
  127.0 0.2 conditional.3
  127.0 0.2 copy.38
  127.2 0.0 copy-start.6
  127.3 0.1 divide_convert_fusion
  127.3 3.1 multiply_reduce_fusion
  130.5 0.0 copy-done.6
  130.5 0.4 convolution_convert_fusion
  130.9 3.0 broadcast_in_dim.74
  133.8 13.3 %all-to-all-start = ((bf16[16,1,80,2048]{3,2,1,0:T(8,128)(2,1)}), bf16[16,1,80,2048]{3,2,1,0:T(8,128)(2,1)}, u32[]{:S(2)}, u32[]{:S(2)}) async-start(bf16[16,1,80,2048]{3,2,1,0:T(8,128)(2,1)} %bitcast.67), calls=%async_computation | async-start | bytes 10485760 | tf_op jit(solution)/shard_map/all_to_all | solution.py:141
  147.2 3.1 pad_maximum_fusion.1
  150.3 0.2 collective-permute-start
  150.4 0.0 copy-start.7
  150.4 4.3 %collective-permute-done = bf16[2,2048,256]{2,1,0:T(8,128)(2,1)} collective-permute-done((bf16[2,2048,256]{2,1,0:T(8,128)(2,1)}, bf16[2,2048,256]{2,1,0:T(8,128)(2,1)}, u32[]{:S(2)}, u32[]{:S(2)}) %collective-permute-start) | collective-permute-done | bytes 2097184 | tf_op jit(solution)/shard_map/ppermute | solution.py:13
  154.8 3.6 pad_maximum_fusion
  158.4 85.2 %all-to-all-done = bf16[16,1,80,2048]{3,2,1,0:T(8,128)(2,1)} async-done(((bf16[16,1,80,2048]{3,2,1,0:T(8,128)(2,1)}), bf16[16,1,80,2048]{3,2,1,0:T(8,128)(2,1)}, u32[]{:S(2)}, u32[]{:S(2)}) %all-to-all-start) | async-done | bytes 5242912 | tf_op jit(solution)/shard_map/all_to_all | solution.py:141
  243.6 0.0 copy-done.7
  243.6 4.0 convolution_reduce_fusion
  247.6 0.0 copy-done
  247.6 11.0 %fusion.57 = f32[1280,2048]{1,0:T(8,128)} fusion(bf16[1,512,2048]{2,1,0:T(8,128)(2,1)S(1)} %copy-done, bf16[1280,2048]{1,0:T(8,128)(2,1)} %bitcast.9, bf16[1,2048,512]{2,1,0:T(8,128)(2,1)} %param.26), kind=kOutput, calls=%fused_computation.75 | convolution fusion | flops 5374607360 | bytes 19922944 | tf_op jit(solution)/shard_map/dot_general | solution.py:150
  258.5 12.2 %add_convert_fusion = bf16[1280,2048]{1,0:T(8,128)(2,1)} fusion(f32[1280,2048]{1,0:T(8,128)} %fusion.57, f32[1280]{0:T(1024)S(1)} %add_divide_fusion, bf16[2,2048,512]{2,1,0:T(8,128)(2,1)} %pad_maximum_fusion, bf16[1280,2048]{1,0:T(8,128)(2,1)} %bitcast.9), kind=kOutput, calls=%fused_computation.47 | convolution fusion | flops 5382471680 | bytes 25170944 | tf_op jit(solution)/shard_map/dot_general | solution.py:151
  270.8 138.5 %all_to_all.8 = bf16[1,16,80,2048]{3,2,0,1:T(8,128)(2,1)S(1)} all-to-all(bf16[1,16,80,2048]{3,2,0,1:T(8,128)(2,1)} %bitcast.71), channel_id=1, replica_groups=mesh['groups'=2,'ctx'=16] {'ctx'}, dimensions={1} | all-to-all | bytes 10485760 | tf_op jit(solution)/shard_map/all_to_all | solution.py:154
  409.2 0.0 copy-start.1
  409.2 1.0 convert_reduce_fusion
  410.2 1.6 fusion.55
  411.7 0.0 copy-done.1
  (3 shorter events, 0.0 us)
Async XLA Ops:
  6.5 241.0 %copy-start = (bf16[1,512,2048]{2,1,0:T(8,128)(2,1)S(1)}, bf16[1,512,2048]{2,1,0:T(8,128)(2,1)}, u32[]{:S(2)}) copy-start(bf16[1,512,2048]{2,1,0:T(8,128)(2,1)} %param.27) | copy-start | bytes 6291460
  6.5 57.9 %all-gather.3.cloned.1.call-start = ((), (), s32[]{:S(2)}) async-start(), calls=%async_computation.2 | async-start | bytes 4456448 | tf_op jit(solution)/shard_map/all_gather | solution.py:58
  8.5 108.8 %all-gather.5.cloned.1.call-start = ((), (), s32[]{:S(2)}) async-start(), calls=%async_computation.3 | async-start | bytes 4456448 | tf_op jit(solution)/shard_map/all_gather | solution.py:59
  117.3 2.8 copy-start.2
  117.5 2.9 copy-start.4
  127.2 3.2 copy-start.6
  133.8 109.8 %all-to-all-start = ((bf16[16,1,80,2048]{3,2,1,0:T(8,128)(2,1)}), bf16[16,1,80,2048]{3,2,1,0:T(8,128)(2,1)}, u32[]{:S(2)}, u32[]{:S(2)}) async-start(bf16[16,1,80,2048]{3,2,1,0:T(8,128)(2,1)} %bitcast.67), calls=%async_computation | async-start | bytes 10485760 | tf_op jit(solution)/shard_map/all_to_all | solution.py:141
  150.3 4.5 %collective-permute-start = (bf16[2,2048,256]{2,1,0:T(8,128)(2,1)}, bf16[2,2048,256]{2,1,0:T(8,128)(2,1)}, u32[]{:S(2)}, u32[]{:S(2)}) collective-permute-start(bf16[2,2048,256]{2,1,0:T(8,128)(2,1)} %pad_maximum_fusion.1), channel_id=1, source_target_pairs={{0,1},{1,0},{2,3},{3,2},{4,5},{5,4},{6,7},{7,6},{8,9},{9,8},{10,11... | collective-permute-start | bytes 6291464 | tf_op jit(solution)/shard_map/ppermute | solution.py:13
  150.4 93.1 %copy-start.7 = (bf16[2048,2]{0,1:T(2,128)(2,1)S(1)}, bf16[2048,2]{0,1:T(2,128)(2,1)}, u32[]{:S(2)}) copy-start(bf16[2048,2]{0,1:T(2,128)(2,1)} %param.24) | copy-start | bytes 24580
  409.2 2.5 copy-start.1
Sparse Core Ops, SparseCore 0:
  9.5 54.9 all-gather.2
  66.6 50.6 all-gather.4
where the time goes:
time: 419 us
  waiting for transfers between devices  195 us (47%)
  blocking collectives  138 us (33%)
  matrix products  36.5 us (9%)
  starting transfers between devices  13.5 us (3%)
  between operations  13.5 us (3%)
  other arithmetic  11.9 us (3%)
  local copies, waits for them, and re-layouts  9.79 us (2%)
    all_to_all x1, blocking collectives, body(): lax.all_to_all(produced.astype(jnp.bfloat16).reshape(received.shape), 'ct...  138 us
    all_to_all x1, waiting for transfers between devices, body(): lax.all_to_all(sending, 'ctx', split_axis=0, concat_axis=1, tiled=True)  85.2 us
    all_gather x1, waiting for transfers between devices, attend(): value_whole = lax.all_gather(values, 'ctx', axis=0, tiled=True)  52.8 us
    all_gather x1, waiting for transfers between devices, attend(): key_whole = lax.all_gather(keys, 'ctx', axis=0, tiled=True)  52.5 us
    all_to_all x1, starting transfers between devices, body(): lax.all_to_all(sending, 'ctx', split_axis=0, concat_axis=1, tiled=True)  13.3 us
    dot_general x1, matrix products, body(): lax.dot_general(mlp_hidden, mlp_blocks[1], (((1,), (1,)), ((), ())), pref...  12.2 us
    dot_general x1, matrix products, body(): jnp.dot(expert_hidden, weight_out, preferred_element_type=jnp.float32)  11 us
  transfers between devices with their start and end apart: 4, of which 4 were waited for; matrix products, arithmetic and copies ran while one was open for 2% of the time, Pallas kernels for 0%

commit v1 on v0

--- a/solution.py
+++ b/solution.py
@@ -56,7 +56,22 @@
     states = tuple(initial)
     key_offset = jnp.int32(0)
     key_whole = lax.all_gather(keys, "ctx", axis=0, tiled=True)
-    value_whole = lax.all_gather(values, "ctx", axis=0, tiled=True)
+
+    def _load_matrix(unit, comm_axis):
+        axis_total = lax.axis_size(comm_axis)
+        blocks_here = []
+        for h in range(axis_total):
+            blocks_here.append((h, (h + 1) % axis_total))
+
+        def _derive_widths(inter):
+            if len(inter) == axis_total:
+                return inter
+            return _derive_widths([lax.ppermute(inter[0], comm_axis, blocks_here), *inter])
+
+        val2 = jnp.concatenate(_derive_widths([unit]), axis=0)
+        return jnp.roll(val2, shift=(lax.axis_index(comm_axis) + 1) * unit.shape[0], axis=0)
+
+    value_whole = _load_matrix(values, "ctx")
     total_keys = key_whole.shape[0]
     step_rows = min(total_keys, 1024)
     for begin in range(0, total_keys, step_rows):

time: 419 us -> 467 us (1.11)
  local copies, waits for them, and re-layouts: 9.79 us -> 29.6 us
  starting transfers between devices: 13.5 us -> 28.1 us
  waiting for transfers between devices: 195 us -> 207 us
    ppermute x0 -> x15, waiting for transfers between devices: none -> 118 us  [_derive_widths(): lax.ppermute(inter[0], comm_axis, blocks_here)]
    all_gather x1 -> x0, waiting for transfers between devices: 52.8 us -> none  [attend(): value_whole = lax.all_gather(values, 'ctx', axis=0, tiled=True)]
    all_gather x1, waiting for transfers between devices: 52.5 us -> 0.01 us  [attend(): key_whole = lax.all_gather(keys, 'ctx', axis=0, tiled=True)]
    unnamed x10 -> x77, local copies, waits for them, and re-layouts: 3.77 us -> 22 us
    ppermute x0 -> x15, starting transfers between devices: none -> 10.4 us  [_derive_widths(): lax.ppermute(inter[0], comm_axis, blocks_here)]
  transfers between devices with their start and end apart: 4 -> 18, of which waited for: 4 -> 17; matrix products, arithmetic and copies ran while one was open for 2% -> 5% of each run, Pallas kernels for 0% -> 0%
where the time goes in v1:
time: 467 us; the launch traced here: 466 us
  waiting for transfers between devices  207 us (44%)
  blocking collectives  138 us (30%)
  matrix products  36.5 us (8%)
  local copies, waits for them, and re-layouts  29.6 us (6%)
  starting transfers between devices  28.1 us (6%)
  between operations  13.9 us (3%)
  other arithmetic  12 us (3%)
    all_to_all x1, blocking collectives, body(): lax.all_to_all(produced.astype(jnp.bfloat16).reshape(received.shape), 'ct...  138 us
    ppermute x15, waiting for transfers between devices, _derive_widths(): lax.ppermute(inter[0], comm_axis, blocks_here)  118 us
    all_to_all x1, waiting for transfers between devices, body(): lax.all_to_all(sending, 'ctx', split_axis=0, concat_axis=1, tiled=True)  85 us
    unnamed x77, local copies, waits for them, and re-layouts  22 us
    all_to_all x1, starting transfers between devices, body(): lax.all_to_all(sending, 'ctx', split_axis=0, concat_axis=1, tiled=True)  17.5 us
    dot_general x1, matrix products, body(): lax.dot_general(mlp_hidden, mlp_blocks[1], (((1,), (1,)), ((), ())), pref...  12.2 us
    dot_general x1, matrix products, body(): jnp.dot(expert_hidden, weight_out, preferred_element_type=jnp.float32)  11 us
    ppermute x15, starting transfers between devices, _derive_widths(): lax.ppermute(inter[0], comm_axis, blocks_here)  10.4 us
  transfers between devices with their start and end apart: 18, of which 17 were waited for; matrix products, arithmetic and copies ran while one was open for 5% of the time, Pallas kernels for 0%

profile of v1, /device:TPU:1, one launch (start us, length us, event | category | flops | bytes accessed | tf_op | source)
XLA Modules:
  0.0 466.1 jit_solution(15907916775263489662)
XLA Ops:
  6.5 1.3 copy.33
  7.8 2.7 collective-permute-start
  10.5 3.3 collective-permute-done
  13.8 2.5 collective-permute-start.1
  16.3 1.8 copy.32
  18.1 1.5 collective-permute-done.1
  19.6 2.5 collective-permute-start.2
  22.1 4.9 %collective-permute-done.2 = bf16[128,1024]{0,1:T(8,128)(2,1)S(1)} collective-permute-done((bf16[128,1024]{0,1:T(8,128)(2,1)S(1)}, bf16[128,1024]{0,1:T(8,128)(2,1)S(1)}, u32[]{:S(2)}, u32[]{:S(2)}) %collective-permute-start.2) | collective-permute-done | bytes 262176 | tf_op jit(solution)/shard_map/ppermute | solution.py:69
  26.9 0.9 collective-permute-start.3
  27.9 7.7 %collective-permute-done.3 = bf16[128,1024]{0,1:T(8,128)(2,1)S(1)} collective-permute-done((bf16[128,1024]{0,1:T(8,128)(2,1)S(1)}, bf16[128,1024]{0,1:T(8,128)(2,1)S(1)}, u32[]{:S(2)}, u32[]{:S(2)}) %collective-permute-start.3) | collective-permute-done | bytes 262176 | tf_op jit(solution)/shard_map/ppermute | solution.py:69
  35.6 0.9 collective-permute-start.4
  36.5 12.8 %collective-permute-done.4 = bf16[128,1024]{0,1:T(8,128)(2,1)S(1)} collective-permute-done((bf16[128,1024]{0,1:T(8,128)(2,1)S(1)}, bf16[128,1024]{0,1:T(8,128)(2,1)S(1)}, u32[]{:S(2)}, u32[]{:S(2)}) %collective-permute-start.4) | collective-permute-done | bytes 262176 | tf_op jit(solution)/shard_map/ppermute | solution.py:69
  49.3 0.7 copy-done.4
  50.0 9.4 %collective-permute-done.5 = bf16[128,1024]{0,1:T(8,128)(2,1)S(1)} collective-permute-done((bf16[128,1024]{0,1:T(8,128)(2,1)S(1)}, bf16[128,1024]{0,1:T(8,128)(2,1)S(1)}, u32[]{:S(2)}, u32[]{:S(2)}) %collective-permute-start.5) | collective-permute-done | bytes 262176 | tf_op jit(solution)/shard_map/ppermute | solution.py:69
  59.4 0.7 copy-done.6
  60.1 0.9 collective-permute-start.6
  61.0 11.6 %collective-permute-done.6 = bf16[128,1024]{0,1:T(8,128)(2,1)S(1)} collective-permute-done((bf16[128,1024]{0,1:T(8,128)(2,1)S(1)}, bf16[128,1024]{0,1:T(8,128)(2,1)S(1)}, u32[]{:S(2)}, u32[]{:S(2)}) %collective-permute-start.6) | collective-permute-done | bytes 262176 | tf_op jit(solution)/shard_map/ppermute | solution.py:69
  72.6 0.7 copy-done.8
  73.3 8.5 %collective-permute-done.7 = bf16[128,1024]{0,1:T(8,128)(2,1)S(1)} collective-permute-done((bf16[128,1024]{0,1:T(8,128)(2,1)S(1)}, bf16[128,1024]{0,1:T(8,128)(2,1)S(1)}, u32[]{:S(2)}, u32[]{:S(2)}) %collective-permute-start.7) | collective-permute-done | bytes 262176 | tf_op jit(solution)/shard_map/ppermute | solution.py:69
  81.8 0.7 copy-done.10
  82.6 8.5 %collective-permute-done.8 = bf16[128,1024]{0,1:T(8,128)(2,1)S(1)} collective-permute-done((bf16[128,1024]{0,1:T(8,128)(2,1)S(1)}, bf16[128,1024]{0,1:T(8,128)(2,1)S(1)}, u32[]{:S(2)}, u32[]{:S(2)}) %collective-permute-start.8) | collective-permute-done | bytes 262176 | tf_op jit(solution)/shard_map/ppermute | solution.py:69
  91.0 0.7 copy-done.12
  91.8 8.5 %collective-permute-done.9 = bf16[128,1024]{0,1:T(8,128)(2,1)S(1)} collective-permute-done((bf16[128,1024]{0,1:T(8,128)(2,1)S(1)}, bf16[128,1024]{0,1:T(8,128)(2,1)S(1)}, u32[]{:S(2)}, u32[]{:S(2)}) %collective-permute-start.9) | collective-permute-done | bytes 262176 | tf_op jit(solution)/shard_map/ppermute | solution.py:69
  100.3 0.7 copy-done.14
  101.0 8.5 %collective-permute-done.10 = bf16[128,1024]{0,1:T(8,128)(2,1)S(1)} collective-permute-done((bf16[128,1024]{0,1:T(8,128)(2,1)S(1)}, bf16[128,1024]{0,1:T(8,128)(2,1)S(1)}, u32[]{:S(2)}, u32[]{:S(2)}) %collective-permute-start.10) | collective-permute-done | bytes 262176 | tf_op jit(solution)/shard_map/ppermute | solution.py:69
  109.5 0.7 copy-done.16
  110.2 8.5 %collective-permute-done.11 = bf16[128,1024]{0,1:T(8,128)(2,1)S(1)} collective-permute-done((bf16[128,1024]{0,1:T(8,128)(2,1)S(1)}, bf16[128,1024]{0,1:T(8,128)(2,1)S(1)}, u32[]{:S(2)}, u32[]{:S(2)}) %collective-permute-start.11) | collective-permute-done | bytes 262176 | tf_op jit(solution)/shard_map/ppermute | solution.py:69
  118.7 0.7 copy-done.18
  119.4 8.5 %collective-permute-done.12 = bf16[128,1024]{0,1:T(8,128)(2,1)S(1)} collective-permute-done((bf16[128,1024]{0,1:T(8,128)(2,1)S(1)}, bf16[128,1024]{0,1:T(8,128)(2,1)S(1)}, u32[]{:S(2)}, u32[]{:S(2)}) %collective-permute-start.12) | collective-permute-done | bytes 262176 | tf_op jit(solution)/shard_map/ppermute | solution.py:69
  127.9 0.7 copy-done.20
  128.6 8.6 %collective-permute-done.13 = bf16[128,1024]{0,1:T(8,128)(2,1)} collective-permute-done((bf16[128,1024]{0,1:T(8,128)(2,1)S(1)}, bf16[128,1024]{0,1:T(8,128)(2,1)}, u32[]{:S(2)}, u32[]{:S(2)}) %collective-permute-start.13) | collective-permute-done | bytes 262176 | tf_op jit(solution)/shard_map/ppermute | solution.py:69
  137.2 0.9 fusion.63
  138.1 0.7 convert_add_fusion
  138.9 7.2 %collective-permute-done.14 = bf16[128,1024]{0,1:T(8,128)(2,1)} collective-permute-done((bf16[128,1024]{0,1:T(8,128)(2,1)}, bf16[128,1024]{0,1:T(8,128)(2,1)}, u32[]{:S(2)}, u32[]{:S(2)}) %collective-permute-start.14) | collective-permute-done | bytes 262176 | tf_op jit(solution)/shard_map/ppermute | solution.py:69
  146.0 1.0 constant_dynamic-update-slice_fusion.31
  147.1 1.0 constant_dynamic-update-slice_fusion.30
  148.1 1.1 constant_dynamic-update-slice_fusion.29
  149.2 1.1 constant_dynamic-update-slice_fusion.28
  150.3 1.1 constant_dynamic-update-slice_fusion.27
  151.5 1.1 constant_dynamic-update-slice_fusion.26
  152.6 1.1 constant_dynamic-update-slice_fusion.25
  153.7 1.1 constant_dynamic-update-slice_fusion.24
  155.6 1.0 constant_dynamic-update-slice_fusion.15
  156.6 1.0 constant_dynamic-update-slice_fusion.14
  159.0 2.3 constant_dynamic-slice_fusion
  161.4 8.8 %conditional.2 = (f32[8,128]{1,0:T(8,128)}, f32[8,128]{1,0:T(8,128)S(1)}, f32[8,128,128]{2,1,0:T(8,128)S(1)}) conditional(s32[]{:T(128)} %convert_element_type.67, () %tuple.20, (s32[]{:T(128)}, bf16[128,1024]{1,0:T(8,128)(2,1)S(1)}, bf16[2048,1024]{0,1:T(8,128)(2,1)}, bf16[2048,1024]{0,1:T(8,128)(2,1)}) %tuple.37), branch_computations={%region_0.1_spmd, %region_1.4_spmd} | conditional | flops 550768768 | bytes 43299896 | solution.py:84
  161.5 1.8 slice.24
  163.3 1.1 fusion
  165.1 2.0 fusion.2
  167.0 0.7 fusion.19
  167.9 2.2 fusion.10
  170.6 3.1 multiply_reduce_fusion
  174.2 3.0 broadcast_in_dim.74
  177.2 17.5 %all-to-all-start = ((bf16[16,1,80,2048]{3,2,1,0:T(8,128)(2,1)}), bf16[16,1,80,2048]{3,2,1,0:T(8,128)(2,1)}, u32[]{:S(2)}, u32[]{:S(2)}) async-start(bf16[16,1,80,2048]{3,2,1,0:T(8,128)(2,1)} %bitcast.67), calls=%async_computation | async-start | bytes 10485760 | tf_op jit(solution)/shard_map/all_to_all | solution.py:156
  194.7 3.1 pad_maximum_fusion.1
  198.0 4.3 collective-permute-done.15
  202.3 3.7 pad_maximum_fusion
  206.0 85.0 %all-to-all-done = bf16[16,1,80,2048]{3,2,1,0:T(8,128)(2,1)} async-done(((bf16[16,1,80,2048]{3,2,1,0:T(8,128)(2,1)}), bf16[16,1,80,2048]{3,2,1,0:T(8,128)(2,1)}, u32[]{:S(2)}, u32[]{:S(2)}) %all-to-all-start) | async-done | bytes 5242912 | tf_op jit(solution)/shard_map/all_to_all | solution.py:156
  291.1 4.0 convolution_reduce_fusion
  295.1 11.0 %fusion.57 = f32[1280,2048]{1,0:T(8,128)} fusion(bf16[1,512,2048]{2,1,0:T(8,128)(2,1)S(1)} %copy-done, bf16[1280,2048]{1,0:T(8,128)(2,1)} %bitcast.9, bf16[1,2048,512]{2,1,0:T(8,128)(2,1)} %param.26), kind=kOutput, calls=%fused_computation.75 | convolution fusion | flops 5374607360 | bytes 19922944 | tf_op jit(solution)/shard_map/dot_general | solution.py:165
  306.1 12.2 %add_convert_fusion = bf16[1280,2048]{1,0:T(8,128)(2,1)} fusion(f32[1280,2048]{1,0:T(8,128)} %fusion.57, f32[1280]{0:T(1024)S(1)} %add_divide_fusion, bf16[2,2048,512]{2,1,0:T(8,128)(2,1)} %pad_maximum_fusion, bf16[1280,2048]{1,0:T(8,128)(2,1)} %bitcast.9), kind=kOutput, calls=%fused_computation.47 | convolution fusion | flops 5382471680 | bytes 25170944 | tf_op jit(solution)/shard_map/dot_general | solution.py:166
  318.3 138.4 %all_to_all.8 = bf16[1,16,80,2048]{3,2,0,1:T(8,128)(2,1)S(1)} all-to-all(bf16[1,16,80,2048]{3,2,0,1:T(8,128)(2,1)} %bitcast.71), channel_id=1, replica_groups=mesh['groups'=2,'ctx'=16] {'ctx'}, dimensions={1} | all-to-all | bytes 10485760 | tf_op jit(solution)/shard_map/all_to_all | solution.py:169
  456.7 1.0 convert_reduce_fusion
  457.7 1.6 fusion.55
  (82 shorter events, 4.1 us)
Async XLA Ops:
  6.5 288.5 %copy-start = (bf16[1,512,2048]{2,1,0:T(8,128)(2,1)S(1)}, bf16[1,512,2048]{2,1,0:T(8,128)(2,1)}, u32[]{:S(2)}) copy-start(bf16[1,512,2048]{2,1,0:T(8,128)(2,1)} %param.27) | copy-start | bytes 6291460
  6.5 154.8 %all-gather.2.cloned.1.call-start = ((), (), s32[]{:S(2)}) async-start(), calls=%async_computation.2 | async-start | bytes 4456448 | tf_op jit(solution)/shard_map/all_gather | solution.py:58
  7.8 6.0 %collective-permute-start = (bf16[128,1024]{0,1:T(8,128)(2,1)S(1)}, bf16[128,1024]{0,1:T(8,128)(2,1)S(1)}, u32[]{:S(2)}, u32[]{:S(2)}) collective-permute-start(bf16[128,1024]{0,1:T(8,128)(2,1)S(1)} %copy.33), channel_id=1, source_target_pairs={{0,1},{1,2},{2,3},{3,4},{4,5},{5,6},{6,7},{7,8},{8,9},{9,10},{10,1... | collective-permute-start | bytes 786440 | tf_op jit(solution)/shard_map/ppermute | solution.py:69
  13.8 5.8 %collective-permute-start.1 = (bf16[128,1024]{0,1:T(8,128)(2,1)S(1)}, bf16[128,1024]{0,1:T(8,128)(2,1)S(1)}, u32[]{:S(2)}, u32[]{:S(2)}) collective-permute-start(bf16[128,1024]{0,1:T(8,128)(2,1)S(1)} %collective-permute-done), channel_id=1, source_target_pairs={{0,1},{1,2},{2,3},{3,4},{4,5},{5,6},{6,7},{7,8},{8,9},{9,10},{10,1... | collective-permute-start | bytes 786440 | tf_op jit(solution)/shard_map/ppermute | solution.py:69
  19.6 7.3 %collective-permute-start.2 = (bf16[128,1024]{0,1:T(8,128)(2,1)S(1)}, bf16[128,1024]{0,1:T(8,128)(2,1)S(1)}, u32[]{:S(2)}, u32[]{:S(2)}) collective-permute-start(bf16[128,1024]{0,1:T(8,128)(2,1)S(1)} %collective-permute-done.1), channel_id=1, source_target_pairs={{0,1},{1,2},{2,3},{3,4},{4,5},{5,6},{6,7},{7,8},{8,9},{9,10},{10,1... | collective-permute-start | bytes 786440 | tf_op jit(solution)/shard_map/ppermute | solution.py:69
  26.9 8.7 %collective-permute-start.3 = (bf16[128,1024]{0,1:T(8,128)(2,1)S(1)}, bf16[128,1024]{0,1:T(8,128)(2,1)S(1)}, u32[]{:S(2)}, u32[]{:S(2)}) collective-permute-start(bf16[128,1024]{0,1:T(8,128)(2,1)S(1)} %collective-permute-done.2), channel_id=1, source_target_pairs={{0,1},{1,2},{2,3},{3,4},{4,5},{5,6},{6,7},{7,8},{8,9},{9,10},{10,1... | collective-permute-start | bytes 786440 | tf_op jit(solution)/shard_map/ppermute | solution.py:69
  35.6 13.7 %collective-permute-start.4 = (bf16[128,1024]{0,1:T(8,128)(2,1)S(1)}, bf16[128,1024]{0,1:T(8,128)(2,1)S(1)}, u32[]{:S(2)}, u32[]{:S(2)}) collective-permute-start(bf16[128,1024]{0,1:T(8,128)(2,1)S(1)} %collective-permute-done.3), channel_id=1, source_target_pairs={{0,1},{1,2},{2,3},{3,4},{4,5},{5,6},{6,7},{7,8},{8,9},{9,10},{10,1... | collective-permute-start | bytes 786440 | tf_op jit(solution)/shard_map/ppermute | solution.py:69
  49.3 0.7 copy-start.4
  50.0 9.4 %collective-permute-start.5 = (bf16[128,1024]{0,1:T(8,128)(2,1)S(1)}, bf16[128,1024]{0,1:T(8,128)(2,1)S(1)}, u32[]{:S(2)}, u32[]{:S(2)}) collective-permute-start(bf16[128,1024]{0,1:T(8,128)(2,1)S(1)} %collective-permute-done.4), channel_id=1, source_target_pairs={{0,1},{1,2},{2,3},{3,4},{4,5},{5,6},{6,7},{7,8},{8,9},{9,10},{10,1... | collective-permute-start | bytes 786440 | tf_op jit(solution)/shard_map/ppermute | solution.py:69
  59.4 0.7 copy-start.6
  60.1 12.5 %collective-permute-start.6 = (bf16[128,1024]{0,1:T(8,128)(2,1)S(1)}, bf16[128,1024]{0,1:T(8,128)(2,1)S(1)}, u32[]{:S(2)}, u32[]{:S(2)}) collective-permute-start(bf16[128,1024]{0,1:T(8,128)(2,1)S(1)} %collective-permute-done.5), channel_id=1, source_target_pairs={{0,1},{1,2},{2,3},{3,4},{4,5},{5,6},{6,7},{7,8},{8,9},{9,10},{10,1... | collective-permute-start | bytes 786440 | tf_op jit(solution)/shard_map/ppermute | solution.py:69
  72.6 0.7 copy-start.8
  73.3 8.5 %collective-permute-start.7 = (bf16[128,1024]{0,1:T(8,128)(2,1)S(1)}, bf16[128,1024]{0,1:T(8,128)(2,1)S(1)}, u32[]{:S(2)}, u32[]{:S(2)}) collective-permute-start(bf16[128,1024]{0,1:T(8,128)(2,1)S(1)} %collective-permute-done.6), channel_id=1, source_target_pairs={{0,1},{1,2},{2,3},{3,4},{4,5},{5,6},{6,7},{7,8},{8,9},{9,10},{10,1... | collective-permute-start | bytes 786440 | tf_op jit(solution)/shard_map/ppermute | solution.py:69
  81.8 0.7 copy-start.10
  82.5 8.5 %collective-permute-start.8 = (bf16[128,1024]{0,1:T(8,128)(2,1)S(1)}, bf16[128,1024]{0,1:T(8,128)(2,1)S(1)}, u32[]{:S(2)}, u32[]{:S(2)}) collective-permute-start(bf16[128,1024]{0,1:T(8,128)(2,1)S(1)} %collective-permute-done.7), channel_id=1, source_target_pairs={{0,1},{1,2},{2,3},{3,4},{4,5},{5,6},{6,7},{7,8},{8,9},{9,10},{10,1... | collective-permute-start | bytes 786440 | tf_op jit(solution)/shard_map/ppermute | solution.py:69
  91.0 0.7 copy-start.12
  91.8 8.5 %collective-permute-start.9 = (bf16[128,1024]{0,1:T(8,128)(2,1)S(1)}, bf16[128,1024]{0,1:T(8,128)(2,1)S(1)}, u32[]{:S(2)}, u32[]{:S(2)}) collective-permute-start(bf16[128,1024]{0,1:T(8,128)(2,1)S(1)} %collective-permute-done.8), channel_id=1, source_target_pairs={{0,1},{1,2},{2,3},{3,4},{4,5},{5,6},{6,7},{7,8},{8,9},{9,10},{10,1... | collective-permute-start | bytes 786440 | tf_op jit(solution)/shard_map/ppermute | solution.py:69
  100.3 0.7 copy-start.14
  101.0 8.5 %collective-permute-start.10 = (bf16[128,1024]{0,1:T(8,128)(2,1)S(1)}, bf16[128,1024]{0,1:T(8,128)(2,1)S(1)}, u32[]{:S(2)}, u32[]{:S(2)}) collective-permute-start(bf16[128,1024]{0,1:T(8,128)(2,1)S(1)} %collective-permute-done.9), channel_id=1, source_target_pairs={{0,1},{1,2},{2,3},{3,4},{4,5},{5,6},{6,7},{7,8},{8,9},{9,10},{10,1... | collective-permute-start | bytes 786440 | tf_op jit(solution)/shard_map/ppermute | solution.py:69
  109.5 0.7 copy-start.16
  110.2 8.5 %collective-permute-start.11 = (bf16[128,1024]{0,1:T(8,128)(2,1)S(1)}, bf16[128,1024]{0,1:T(8,128)(2,1)S(1)}, u32[]{:S(2)}, u32[]{:S(2)}) collective-permute-start(bf16[128,1024]{0,1:T(8,128)(2,1)S(1)} %collective-permute-done.10), channel_id=1, source_target_pairs={{0,1},{1,2},{2,3},{3,4},{4,5},{5,6},{6,7},{7,8},{8,9},{9,10},{10,1... | collective-permute-start | bytes 786440 | tf_op jit(solution)/shard_map/ppermute | solution.py:69
  118.7 0.7 copy-start.18
  119.4 8.5 %collective-permute-start.12 = (bf16[128,1024]{0,1:T(8,128)(2,1)S(1)}, bf16[128,1024]{0,1:T(8,128)(2,1)S(1)}, u32[]{:S(2)}, u32[]{:S(2)}) collective-permute-start(bf16[128,1024]{0,1:T(8,128)(2,1)S(1)} %collective-permute-done.11), channel_id=1, source_target_pairs={{0,1},{1,2},{2,3},{3,4},{4,5},{5,6},{6,7},{7,8},{8,9},{9,10},{10,1... | collective-permute-start | bytes 786440 | tf_op jit(solution)/shard_map/ppermute | solution.py:69
  127.9 0.7 copy-start.20
  128.6 8.6 %collective-permute-start.13 = (bf16[128,1024]{0,1:T(8,128)(2,1)S(1)}, bf16[128,1024]{0,1:T(8,128)(2,1)}, u32[]{:S(2)}, u32[]{:S(2)}) collective-permute-start(bf16[128,1024]{0,1:T(8,128)(2,1)S(1)} %collective-permute-done.12), channel_id=1, source_target_pairs={{0,1},{1,2},{2,3},{3,4},{4,5},{5,6},{6,7},{7,8},{8,9},{9,10},{10,1... | collective-permute-start | bytes 786440 | tf_op jit(solution)/shard_map/ppermute | solution.py:69
  137.2 8.8 %collective-permute-start.14 = (bf16[128,1024]{0,1:T(8,128)(2,1)}, bf16[128,1024]{0,1:T(8,128)(2,1)}, u32[]{:S(2)}, u32[]{:S(2)}) collective-permute-start(bf16[128,1024]{0,1:T(8,128)(2,1)} %collective-permute-done.13), channel_id=1, source_target_pairs={{0,1},{1,2},{2,3},{3,4},{4,5},{5,6},{6,7},{7,8},{8,9},{9,10},{10,1... | collective-permute-start | bytes 786440 | tf_op jit(solution)/shard_map/ppermute | solution.py:69
  138.1 16.7 %copy-start.9 = (bf16[128,1024]{0,1:T(8,128)(2,1)S(1)}, bf16[128,1024]{0,1:T(8,128)(2,1)}, u32[]{:S(2)}) copy-start(bf16[128,1024]{0,1:T(8,128)(2,1)} %copy-done.8) | copy-start | bytes 786436
  138.1 16.8 %copy-start.7 = (bf16[128,1024]{0,1:T(8,128)(2,1)S(1)}, bf16[128,1024]{0,1:T(8,128)(2,1)}, u32[]{:S(2)}) copy-start(bf16[128,1024]{0,1:T(8,128)(2,1)} %copy-done.6) | copy-start | bytes 786436
  138.1 16.9 %copy-start.5 = (bf16[128,1024]{0,1:T(8,128)(2,1)S(1)}, bf16[128,1024]{0,1:T(8,128)(2,1)}, u32[]{:S(2)}) copy-start(bf16[128,1024]{0,1:T(8,128)(2,1)} %copy-done.4) | copy-start | bytes 786436
  148.1 9.6 %copy-start.21 = (bf16[128,1024]{0,1:T(8,128)(2,1)S(1)}, bf16[128,1024]{0,1:T(8,128)(2,1)}, u32[]{:S(2)}) copy-start(bf16[128,1024]{0,1:T(8,128)(2,1)} %copy-done.20) | copy-start | bytes 786436
  149.2 8.5 %copy-start.19 = (bf16[128,1024]{0,1:T(8,128)(2,1)S(1)}, bf16[128,1024]{0,1:T(8,128)(2,1)}, u32[]{:S(2)}) copy-start(bf16[128,1024]{0,1:T(8,128)(2,1)} %copy-done.18) | copy-start | bytes 786436
  150.3 7.5 %copy-start.17 = (bf16[128,1024]{0,1:T(8,128)(2,1)S(1)}, bf16[128,1024]{0,1:T(8,128)(2,1)}, u32[]{:S(2)}) copy-start(bf16[128,1024]{0,1:T(8,128)(2,1)} %copy-done.16) | copy-start | bytes 786436
  151.4 6.5 %copy-start.15 = (bf16[128,1024]{0,1:T(8,128)(2,1)S(1)}, bf16[128,1024]{0,1:T(8,128)(2,1)}, u32[]{:S(2)}) copy-start(bf16[128,1024]{0,1:T(8,128)(2,1)} %copy-done.14) | copy-start | bytes 786436
  152.6 5.5 %copy-start.13 = (bf16[128,1024]{0,1:T(8,128)(2,1)S(1)}, bf16[128,1024]{0,1:T(8,128)(2,1)}, u32[]{:S(2)}) copy-start(bf16[128,1024]{0,1:T(8,128)(2,1)} %copy-done.12) | copy-start | bytes 786436
  153.7 4.5 copy-start.11
  159.0 2.3 copy-start.3
  163.3 4.4 copy-start.1
  170.6 3.2 copy-start.22
  177.2 113.9 %all-to-all-start = ((bf16[16,1,80,2048]{3,2,1,0:T(8,128)(2,1)}), bf16[16,1,80,2048]{3,2,1,0:T(8,128)(2,1)}, u32[]{:S(2)}, u32[]{:S(2)}) async-start(bf16[16,1,80,2048]{3,2,1,0:T(8,128)(2,1)} %bitcast.67), calls=%async_computation | async-start | bytes 10485760 | tf_op jit(solution)/shard_map/all_to_all | solution.py:156
  197.8 4.5 collective-permute-start.15
  198.0 93.1 %copy-start.23 = (bf16[2048,2]{0,1:T(2,128)(2,1)S(1)}, bf16[2048,2]{0,1:T(2,128)(2,1)}, u32[]{:S(2)}) copy-start(bf16[2048,2]{0,1:T(2,128)(2,1)} %param.24) | copy-start | bytes 24580
Sparse Core Ops, SparseCore 0:
  18.2 58.4 all-gather.1
